TPU v7x, 128 devices: a whole 4x4x4 slice. The times are simulated.
128 devices in a mesh: prompt: 4 (over z_hi, core), resp: 32 (over y, x, z_lo).
Axes of the slice: x: 4, y: 4, z: 4 (z_hi: 2, z_lo: 2; z = z_hi * 2 + z_lo), core: 2. Of those that a mesh axis runs over, the one named last changes fastest.
Arguments:
- queries: bfloat16 [4, 4096, 8192], P('prompt', 'resp'), may hold values from -6 to 6
- resp_kv: bfloat16 [4, 4096, 2048], P('prompt', 'resp'), may hold values from -6 to 6
- resp_segments: int32 [4, 4096], P('prompt', 'resp'), may hold values from 0 to 7, never falling along the last dimension, each value on 1 to 896 neighbouring positions
- prefix_kv: bfloat16 [512, 8, 2048], P(('prompt', 'resp')), may hold values from -6 to 6
- tile_plan: int32 [512, 2], P(('prompt', 'resp')), may hold values from 0 to 127, as said below
- prompt_lengths: int32 [4], P('prompt'), may hold values from 8 to 1024
Outputs:
- attended: bfloat16 [4, 4096, 8192], P('prompt', 'resp')
Inputs may be any that keep to these rules, and one draw needn't show every extreme that they name: `tile_plan`: column 0 is a group in 0 .. 3 and column 1 a place in 0 .. 127; each pair of group and place stands once; the 4 tiles of each device hold one tile of every group, in any order. `resp_segments`: response numbers never fall along a group's tokens; each response has 1 to 896 tokens.
All inputs are finite; a program needn't handle non-finite values.
Results may differ from a plain program's by a relative error of at most 0.0055.
Values may be sent and summed in bfloat16 or wider, within the bound.
A program may use at most 128 MiB of HBM per device.

v0:
```python
import math
import jax
import jax.numpy as jnp
from jax import lax
from jax.sharding import PartitionSpec as P

H = 64
KVH = 8
HD = 128
NEG_FILL = -1e30


def passed_along(value, axis, steps):
    count = lax.axis_size(axis)
    first, last = (max(0, -steps), min(count, count - steps))
    return lax.ppermute(value, axis, [(source, source + steps) for source in range(first, last)])


def absorb(carry, query_head_rows, key_vectors, value_vectors, visible, score_scale):
    running, total, weighted_sum = carry
    logit_scores = (
        jnp.einsum(
            "wcpo,lco->wcpl", query_head_rows, key_vectors, preferred_element_type=jnp.float32
        )
        * score_scale
    )
    logit_scores = jnp.where(visible, logit_scores, NEG_FILL)
    fresh = jnp.maximum(running, jnp.max(logit_scores, axis=-1))
    factor = jnp.exp(running - fresh)
    attention_weight = jnp.where(visible, jnp.exp(logit_scores - fresh[..., None]), 0.0)
    total = total * factor + jnp.sum(attention_weight, axis=-1)
    update = jnp.einsum(
        "luem,mut->luet",
        attention_weight.astype(jnp.bfloat16),
        value_vectors,
        preferred_element_type=jnp.float32,
    )
    weighted_sum = weighted_sum * factor[..., None] + update
    return (fresh, total, weighted_sum)


def on_device(queries, resp_kv, resp_segments, prefix_kv, tile_plan, prompt_lengths):
    rows = queries.shape[1]
    heads_kv = KVH
    width = HD
    group_size = H // KVH
    split = heads_kv * width
    score_scale = 1.0 / math.sqrt(width)
    reach = 7
    query_head_rows = queries[0].reshape(rows, heads_kv, group_size, width)
    own_kv = resp_kv[0]
    own_seg = resp_segments[0] + 1
    key_vectors = own_kv[:, :split].reshape(rows, heads_kv, width)
    value_vectors = own_kv[:, split:].reshape(rows, heads_kv, width)
    query_pos = jnp.arange(rows, dtype=jnp.int32)
    visible = (own_seg[None, :] == own_seg[:, None]) & (query_pos[None, :] <= query_pos[:, None])
    start_state = (
        jnp.full((rows, heads_kv, group_size), NEG_FILL, jnp.float32),
        jnp.zeros((rows, heads_kv, group_size), jnp.float32),
        jnp.zeros((rows, heads_kv, group_size, width), jnp.float32),
    )
    carry = absorb(
        start_state,
        query_head_rows,
        key_vectors,
        value_vectors,
        visible[:, None, None, :],
        score_scale,
    )
    moving = (own_kv, own_seg)
    for step in range(reach):
        moving = passed_along((moving[0], moving[1]), "resp", 1)
        block_kv = moving[0]
        seen = own_seg[:, None] == moving[1][None, :]

        def absorb_update(current):
            block_keys = block_kv[:, :split].reshape(-1, heads_kv, width)
            block_values = block_kv[:, split:].reshape(-1, heads_kv, width)
            return absorb(
                current,
                query_head_rows,
                block_keys,
                block_values,
                seen[:, None, None, :],
                score_scale,
            )

        carry = lax.cond(jnp.any(seen), absorb_update, lambda current: current, carry)
    group = lax.axis_index("prompt")
    limit = prompt_lengths[0]
    n_prompt = lax.axis_size("prompt")
    state = carry
    tiles = lax.all_gather(prefix_kv, ("prompt", "resp"), axis=0, tiled=True)
    plan = lax.all_gather(tile_plan, ("prompt", "resp"), axis=0, tiled=True)
    count = tiles.shape[0]
    tile = tiles.shape[1]
    count = count // n_prompt
    order = jnp.argsort(jnp.where(plan[:, 0] == group, 0, 1), stable=True)[:count]
    tiles = tiles[order]
    plan = plan[order]
    cap = max(1, 512 // tile)
    per = max((d for d in range(1, min(count, cap) + 1) if count % d == 0))
    places = plan[:, 1][:, None] * tile + jnp.arange(tile, dtype=jnp.int32)[None, :]
    live = (places < limit).reshape(count // per, per * tile)
    blocks = tiles.reshape(count // per, per * tile, tiles.shape[2])

    def advance(inner, item):
        block, mask = item

        def update(current):
            block_keys = block[:, :split].reshape(-1, heads_kv, width)
            block_values = block[:, split:].reshape(-1, heads_kv, width)
            return absorb(
                current,
                query_head_rows,
                block_keys,
                block_values,
                mask[None, None, None, :],
                score_scale,
            )

        return (lax.cond(jnp.any(mask), update, lambda current: current, inner), None)

    state, _ = lax.scan(advance, state, (blocks, live))
    carry = state
    running, total, weighted_sum = carry
    result = (weighted_sum / total[..., None]).reshape(rows, H * HD).astype(jnp.bfloat16)
    return result[None]


def solution(mesh):
    return jax.shard_map(
        on_device,
        mesh=mesh,
        in_specs=(
            P("prompt", "resp", None),
            P("prompt", "resp", None),
            P("prompt", "resp"),
            P(("prompt", "resp"), None, None),
            P(("prompt", "resp"), None),
            P("prompt"),
        ),
        out_specs=P("prompt", "resp", None),
        check_vma=False,
    )
```

profile of v0, /device:TPU:89, one launch (start us, length us, event | category | flops | bytes accessed | tf_op | source)
XLA Modules:
  0.0 580.5 jit_solution(3379956316032789623)
XLA Ops:
  11.8 14.5 %collective-permute-done.7 = bf16[128,2048]{0,1:T(8,128)(2,1)S(1)} collective-permute-done((bf16[128,2048]{0,1:T(8,128)(2,1)S(1)}, bf16[128,2048]{0,1:T(8,128)(2,1)S(1)}, u32[]{:S(2)}, u32[]{:S(2)}) %collective-permute-start.7) | collective-permute-done | bytes 524320 | tf_op jit(solution)/shard_map/ppermute | solution.py:16
  28.2 14.9 %collective-permute-done.8 = bf16[128,2048]{0,1:T(8,128)(2,1)S(1)} collective-permute-done((bf16[128,2048]{0,1:T(8,128)(2,1)S(1)}, bf16[128,2048]{0,1:T(8,128)(2,1)S(1)}, u32[]{:S(2)}, u32[]{:S(2)}) %collective-permute-start.8) | collective-permute-done | bytes 524320 | tf_op jit(solution)/shard_map/ppermute | solution.py:16
  51.0 8.1 %collective-permute-done = s32[128]{0:T(128)S(1)} collective-permute-done((s32[128]{0:T(128)S(1)}, s32[128]{0:T(128)S(1)}, u32[]{:S(2)}, u32[]{:S(2)}) %collective-permute-start) | collective-permute-done | bytes 544 | tf_op jit(solution)/shard_map/ppermute | solution.py:16
  61.4 291.9 %all-gather = s32[128,4,2]{1,2,0:T(2,128)S(1)} all-gather(s32[1,4,2]{1,2,0:T(2,128)} %bitcast.282), channel_id=1, replica_groups=mesh['prompt'=4,'resp'=32] {'prompt','resp'}, dimensions={0}, use_global_device_ids=true | all-gather | bytes 4128 | tf_op jit(solution)/shard_map/all_gather | solution.py:94
  361.7 7.3 %collective-permute-start.3 = (s32[128]{0:T(128)S(1)}, s32[128]{0:T(128)S(1)}, u32[]{:S(2)}, u32[]{:S(2)}) collective-permute-start(s32[128]{0:T(128)S(1)} %collective-permute-done.2), channel_id=1, source_target_pairs={{0,1},{1,2},{2,3},{3,4},{4,5},{5,6},{6,7},{7,8},{8,9},{9,10},{10,1... | collective-permute-start | bytes 1544 | tf_op jit(solution)/shard_map/ppermute | solution.py:16
  372.7 7.5 %collective-permute-start.4 = (s32[128]{0:T(128)S(1)}, s32[128]{0:T(128)S(1)}, u32[]{:S(2)}, u32[]{:S(2)}) collective-permute-start(s32[128]{0:T(128)S(1)} %collective-permute-done.3), channel_id=1, source_target_pairs={{0,1},{1,2},{2,3},{3,4},{4,5},{5,6},{6,7},{7,8},{8,9},{9,10},{10,1... | collective-permute-start | bytes 1544 | tf_op jit(solution)/shard_map/ppermute | solution.py:16
  383.1 6.0 %collective-permute-start.5 = (s32[128]{0:T(128)S(1)}, s32[128]{0:T(128)S(1)}, u32[]{:S(2)}, u32[]{:S(2)}) collective-permute-start(s32[128]{0:T(128)S(1)} %collective-permute-done.4), channel_id=1, source_target_pairs={{0,1},{1,2},{2,3},{3,4},{4,5},{5,6},{6,7},{7,8},{8,9},{9,10},{10,1... | collective-permute-start | bytes 1544 | tf_op jit(solution)/shard_map/ppermute | solution.py:16
  409.1 9.0 %collective-permute-done.11 = bf16[128,2048]{0,1:T(8,128)(2,1)S(1)} collective-permute-done((bf16[128,2048]{0,1:T(8,128)(2,1)}, bf16[128,2048]{0,1:T(8,128)(2,1)S(1)}, u32[]{:S(2)}, u32[]{:S(2)}) %collective-permute-start.11) | collective-permute-done | bytes 524320 | tf_op jit(solution)/shard_map/ppermute | solution.py:16
  423.7 7.5 %collective-permute-done.12 = bf16[128,2048]{0,1:T(8,128)(2,1)} collective-permute-done((bf16[128,2048]{0,1:T(8,128)(2,1)S(1)}, bf16[128,2048]{0,1:T(8,128)(2,1)}, u32[]{:S(2)}, u32[]{:S(2)}) %collective-permute-start.12) | collective-permute-done | bytes 524320 | tf_op jit(solution)/shard_map/ppermute | solution.py:16
  437.5 5.3 bitcast_add_fusion.8
  442.8 8.4 %conditional.8 = ((f32[128,8,8]{0,2,1:T(8,128)S(1)}, f32[128,8,8]{0,2,1:T(8,128)S(1)}, f32[128,8,8,128]{3,0,2,1:T(8,128)})) conditional(s32[]{:T(128)} %convert_element_type.71, (f32[128,8,8]{0,2,1:T(8,128)S(1)}, f32[128,8,8]{0,2,1:T(8,128)S(1)}, f32[128,8,8,128]{3,0,2,1:T(8,128)}) %tuple.61, (pred[128,128]{0,1:T(8,128)(4,1)S(1)}, ...), branch_computations={%region_9.10_spmd, %region_10.13_spmd} | conditional | flops 552615936 | bytes 25215008 | solution.py:88
  446.0 5.3 bitcast_add_fusion
  451.2 8.9 %conditional.9 = ((f32[128,8,8]{0,2,1:T(8,128)S(1)}, f32[128,8,8]{0,2,1:T(8,128)S(1)}, f32[128,8,8,128]{3,0,2,1:T(8,128)})) conditional(s32[]{:T(128)} %convert_element_type.70, (f32[128,8,8]{0,2,1:T(8,128)S(1)}, f32[128,8,8]{0,2,1:T(8,128)S(1)}, f32[128,8,8,128]{3,0,2,1:T(8,128)}) %get-tuple-element.662, (pred[128,128]{0,1:T(8,128)(4,1)S(1)}, ...), branch_computations={%region_13.14_spmd, %region_14.17_spmd} | conditional | flops 552615936 | bytes 25215008 | solution.py:88
  454.8 5.3 bitcast_add_fusion.1
  460.1 7.4 %conditional.10 = ((f32[128,8,8]{0,2,1:T(8,128)S(1)}, f32[128,8,8]{0,2,1:T(8,128)S(1)}, f32[128,8,8,128]{3,0,2,1:T(8,128)})) conditional(s32[]{:T(128)} %convert_element_type.69, (f32[128,8,8]{0,2,1:T(8,128)S(1)}, f32[128,8,8]{0,2,1:T(8,128)S(1)}, f32[128,8,8,128]{3,0,2,1:T(8,128)}) %get-tuple-element.663, (pred[128,128]{0,1:T(8,128)(4,1)S(1)}, ...), branch_computations={%region_17.18_spmd, %region_18.21_spmd} | conditional | flops 552615936 | bytes 25215008 | solution.py:88
  462.2 5.3 bitcast_add_fusion.2
  467.5 8.5 %conditional.11 = ((f32[128,8,8]{0,2,1:T(8,128)S(1)}, f32[128,8,8]{0,2,1:T(8,128)S(1)}, f32[128,8,8,128]{3,0,2,1:T(8,128)})) conditional(s32[]{:T(128)} %convert_element_type.68, (f32[128,8,8]{0,2,1:T(8,128)S(1)}, f32[128,8,8]{0,2,1:T(8,128)S(1)}, f32[128,8,8,128]{3,0,2,1:T(8,128)}) %get-tuple-element.664, (pred[128,128]{0,1:T(8,128)(4,1)S(1)}, ...), branch_computations={%region_21.0_spmd, %region_22.25_spmd} | conditional | flops 552615936 | bytes 25215008 | solution.py:88
  470.7 5.3 bitcast_add_fusion.3
  476.0 7.6 %conditional.12 = ((f32[128,8,8]{0,2,1:T(8,128)S(1)}, f32[128,8,8]{0,2,1:T(8,128)S(1)}, f32[128,8,8,128]{3,0,2,1:T(8,128)})) conditional(s32[]{:T(128)} %convert_element_type.67, (f32[128,8,8]{0,2,1:T(8,128)S(1)}, f32[128,8,8]{0,2,1:T(8,128)S(1)}, f32[128,8,8,128]{3,0,2,1:T(8,128)}) %get-tuple-element.665, (pred[128,128]{0,1:T(8,128)(4,1)S(1)}, ...), branch_computations={%region_25.0_spmd, %region_26.29_spmd} | conditional | flops 552615936 | bytes 25215008 | solution.py:88
  478.3 5.3 bitcast_add_fusion.4
  483.6 8.4 %conditional.13 = ((f32[128,8,8]{0,2,1:T(8,128)S(1)}, f32[128,8,8]{0,2,1:T(8,128)S(1)}, f32[128,8,8,128]{3,0,2,1:T(8,128)})) conditional(s32[]{:T(128)} %convert_element_type.66, (f32[128,8,8]{0,2,1:T(8,128)S(1)}, f32[128,8,8]{0,2,1:T(8,128)S(1)}, f32[128,8,8,128]{3,0,2,1:T(8,128)}) %get-tuple-element.666, (pred[128,128]{0,1:T(8,128)(4,1)S(1)}, ...), branch_computations={%region_29.30_spmd, %region_30.33_spmd} | conditional | flops 552615936 | bytes 25215008 | solution.py:88
  486.7 5.3 bitcast_add_fusion.5
  492.0 7.6 %conditional.14 = ((f32[128,8,8]{0,2,1:T(8,128)S(1)}, f32[128,8,8]{0,2,1:T(8,128)S(1)}, f32[128,8,8,128]{3,0,2,1:T(8,128)})) conditional(s32[]{:T(128)} %convert_element_type.65, (f32[128,8,8]{0,2,1:T(8,128)S(1)}, f32[128,8,8]{0,2,1:T(8,128)S(1)}, f32[128,8,8,128]{3,0,2,1:T(8,128)}) %get-tuple-element.667, (pred[128,128]{0,1:T(8,128)(4,1)S(1)}, ...), branch_computations={%region_33.34_spmd, %region_34.37_spmd} | conditional | flops 552615936 | bytes 25215008 | solution.py:88
  494.2 5.3 bitcast_add_fusion.6
  499.6 8.6 %gather_fusion.1 = bf16[128,8,2048]{2,1,0:T(8,128)(2,1)} fusion(bf16[512,8,2048]{2,1,0:T(8,128)(2,1)} %all-gather.3.cloned.1.call-done, s32[1024]{0:T(1024)S(1)} %pad_clamp_fusion), kind=kCustom, calls=%fused_computation.1 | custom fusion | bytes 8389120 | tf_op jit(solution)/shard_map/gather | solution.py:99
  508.2 6.4 %copy.137 = bf16[2,512,2048]{1,2,0:T(8,128)(2,1)} copy(bf16[2,512,2048]{2,1,0:T(8,128)(2,1)} %bitcast.261) | data formatting | bytes 8388608 | tf_op jit(solution)/shard_map/while | solution.py:124
  514.6 49.1 %while.14 = (s32[]{:T(128)}, f32[128,8,8]{0,2,1:T(8,128)S(1)}, f32[128,8,8]{0,2,1:T(8,128)S(1)}, f32[128,8,8,128]{3,0,2,1:T(8,128)}, pred[2,512]{1,0:T(4,128)(4,...) while((s32[]{:T(128)}, f32[128,8,8]{0,2,1:T(8,128)S(1)}, ...), condition=%wide.region_44.45_spmd, body=%wide.region_38.44_spmd.sunk | while | flops 2204123648 | bytes 138940144 | solution.py:124
  515.9 23.3 %conditional.16 = ((f32[128,8,8]{0,2,1:T(8,128)S(1)}, f32[128,8,8]{0,2,1:T(8,128)S(1)}, f32[128,8,8,128]{3,0,2,1:T(8,128)})) conditional(s32[]{:T(128)} %convert_element_type.97, (f32[128,8,8]{0,2,1:T(8,128)S(1)}, f32[128,8,8]{0,2,1:T(8,128)S(1)}, f32[128,8,8,128]{3,0,2,1:T(8,128)}) %tuple.148, (pred[1,512]{1,0:T(4,128)(4,1)S(1)}, ...), branch_computations={%region_40.40_spmd, %region_41.43_spmd} | conditional | flops 2204123136 | bytes 138938944 | solution.py:122
  527.6 11.6 %bitcast_add_fusion.7 = f32[128,8,8,128]{3,0,2,1:T(8,128)} fusion(f32[128,8,8,128]{3,0,2,1:T(8,128)} %get-tuple-element.245, bf16[512,8,128,1]{0,2,3,1:T(8,128)(2,1)S(1)} %bitcast.260, f32[8,512,128,8]{2,1,3,0:T(8,128)} %copy-done, f32[128,8,8]{0,2,1:T(8,128)S(1)} %max.24, pred[512]{0:T(512)(128)(4,1)S(1)} %reduce.1, f32[128,8,8]{0,2,1:T(8,128)S(1)} %get-tuple-element.488), kind=kOutput, calls=%fused_computation.124 | convolution fusion | flops 1096810496 | bytes 26280448 | tf_op jit(solution)/shard_map/while/body/eval_jaxpr/cond/branch_1_fun/luem,mut->luet/dot_general | solution.py:32
  540.4 23.3 %conditional.16 = ((f32[128,8,8]{0,2,1:T(8,128)S(1)}, f32[128,8,8]{0,2,1:T(8,128)S(1)}, f32[128,8,8,128]{3,0,2,1:T(8,128)})) conditional(s32[]{:T(128)} %convert_element_type.97, (f32[128,8,8]{0,2,1:T(8,128)S(1)}, f32[128,8,8]{0,2,1:T(8,128)S(1)}, f32[128,8,8,128]{3,0,2,1:T(8,128)}) %tuple.148, (pred[1,512]{1,0:T(4,128)(4,1)S(1)}, ...), branch_computations={%region_40.40_spmd, %region_41.43_spmd} | conditional | flops 2204123136 | bytes 138938944 | solution.py:122
  546.4 4.9 fusion.87
  552.2 11.6 %bitcast_add_fusion.7 = f32[128,8,8,128]{3,0,2,1:T(8,128)} fusion(f32[128,8,8,128]{3,0,2,1:T(8,128)} %get-tuple-element.245, bf16[512,8,128,1]{0,2,3,1:T(8,128)(2,1)S(1)} %bitcast.260, f32[8,512,128,8]{2,1,3,0:T(8,128)} %copy-done, f32[128,8,8]{0,2,1:T(8,128)S(1)} %max.24, pred[512]{0:T(512)(128)(4,1)S(1)} %reduce.1, f32[128,8,8]{0,2,1:T(8,128)S(1)} %get-tuple-element.488), kind=kOutput, calls=%fused_computation.124 | convolution fusion | flops 1096810496 | bytes 26280448 | tf_op jit(solution)/shard_map/while/body/eval_jaxpr/cond/branch_1_fun/luem,mut->luet/dot_general | solution.py:32
  (123 shorter events, 107.2 us)
Async XLA Ops:
  6.5 493.1 %all-gather.3.cloned.1.call-start = ((), (), s32[]{:S(2)}) async-start(), calls=%async_computation | async-start | bytes 16908288 | tf_op jit(solution)/shard_map/all_gather | solution.py:93
  8.6 17.8 %collective-permute-start.7 = (bf16[128,2048]{0,1:T(8,128)(2,1)S(1)}, bf16[128,2048]{0,1:T(8,128)(2,1)S(1)}, u32[]{:S(2)}, u32[]{:S(2)}) collective-permute-start(bf16[128,2048]{0,1:T(8,128)(2,1)S(1)} %bitcast.264), channel_id=1, source_target_pairs={{0,1},{1,2},{2,3},{3,4},{4,5},{5,6},{6,7},{7,8},{8,9},{9,10},{10,1... | collective-permute-start | bytes 1572872 | tf_op jit(solution)/shard_map/ppermute | solution.py:16
  26.3 368.8 %copy-start.5 = (bf16[128,2048]{0,1:T(8,128)(2,1)}, bf16[128,2048]{0,1:T(8,128)(2,1)S(1)}, u32[]{:S(2)}) copy-start(bf16[128,2048]{0,1:T(8,128)(2,1)S(1)} %collective-permute-done.7) | copy-start | bytes 1572868
  26.3 16.8 %collective-permute-start.8 = (bf16[128,2048]{0,1:T(8,128)(2,1)S(1)}, bf16[128,2048]{0,1:T(8,128)(2,1)S(1)}, u32[]{:S(2)}, u32[]{:S(2)}) collective-permute-start(bf16[128,2048]{0,1:T(8,128)(2,1)S(1)} %collective-permute-done.7), channel_id=1, source_target_pairs={{0,1},{1,2},{2,3},{3,4},{4,5},{5,6},{6,7},{7,8},{8,9},{9,10},{10,1... | collective-permute-start | bytes 1572872 | tf_op jit(solution)/shard_map/ppermute | solution.py:16
  43.2 352.0 %copy-start.4 = (bf16[128,2048]{0,1:T(8,128)(2,1)}, bf16[128,2048]{0,1:T(8,128)(2,1)S(1)}, u32[]{:S(2)}) copy-start(bf16[128,2048]{0,1:T(8,128)(2,1)S(1)} %collective-permute-done.8) | copy-start | bytes 1572868
  43.2 325.9 %collective-permute-start.9 = (bf16[128,2048]{0,1:T(8,128)(2,1)S(1)}, bf16[128,2048]{0,1:T(8,128)(2,1)S(1)}, u32[]{:S(2)}, u32[]{:S(2)}) collective-permute-start(bf16[128,2048]{0,1:T(8,128)(2,1)S(1)} %collective-permute-done.8), channel_id=1, source_target_pairs={{0,1},{1,2},{2,3},{3,4},{4,5},{5,6},{6,7},{7,8},{8,9},{9,10},{10,1... | collective-permute-start | bytes 1572872 | tf_op jit(solution)/shard_map/ppermute | solution.py:16
  45.7 13.4 %collective-permute-start = (s32[128]{0:T(128)S(1)}, s32[128]{0:T(128)S(1)}, u32[]{:S(2)}, u32[]{:S(2)}) collective-permute-start(s32[128]{0:T(128)S(1)} %add_bitcast_fusion), channel_id=1, source_target_pairs={{0,1},{1,2},{2,3},{3,4},{4,5},{5,6},{6,7},{7,8},{8,9},{9,10},{10,1... | collective-permute-start | bytes 1544 | tf_op jit(solution)/shard_map/ppermute | solution.py:16
  59.1 295.0 %collective-permute-start.1 = (s32[128]{0:T(128)S(1)}, s32[128]{0:T(128)S(1)}, u32[]{:S(2)}, u32[]{:S(2)}) collective-permute-start(s32[128]{0:T(128)S(1)} %collective-permute-done), channel_id=1, source_target_pairs={{0,1},{1,2},{2,3},{3,4},{4,5},{5,6},{6,7},{7,8},{8,9},{9,10},{10,1... | collective-permute-start | bytes 1544 | tf_op jit(solution)/shard_map/ppermute | solution.py:16
  354.2 7.5 %collective-permute-start.2 = (s32[128]{0:T(128)S(1)}, s32[128]{0:T(128)S(1)}, u32[]{:S(2)}, u32[]{:S(2)}) collective-permute-start(s32[128]{0:T(128)S(1)} %collective-permute-done.1), channel_id=1, source_target_pairs={{0,1},{1,2},{2,3},{3,4},{4,5},{5,6},{6,7},{7,8},{8,9},{9,10},{10,1... | collective-permute-start | bytes 1544 | tf_op jit(solution)/shard_map/ppermute | solution.py:16
  361.7 11.0 %collective-permute-start.3 = (s32[128]{0:T(128)S(1)}, s32[128]{0:T(128)S(1)}, u32[]{:S(2)}, u32[]{:S(2)}) collective-permute-start(s32[128]{0:T(128)S(1)} %collective-permute-done.2), channel_id=1, source_target_pairs={{0,1},{1,2},{2,3},{3,4},{4,5},{5,6},{6,7},{7,8},{8,9},{9,10},{10,1... | collective-permute-start | bytes 1544 | tf_op jit(solution)/shard_map/ppermute | solution.py:16
  369.1 32.0 %collective-permute-start.10 = (bf16[128,2048]{0,1:T(8,128)(2,1)S(1)}, bf16[128,2048]{0,1:T(8,128)(2,1)}, u32[]{:S(2)}, u32[]{:S(2)}) collective-permute-start(bf16[128,2048]{0,1:T(8,128)(2,1)S(1)} %collective-permute-done.9), channel_id=1, source_target_pairs={{0,1},{1,2},{2,3},{3,4},{4,5},{5,6},{6,7},{7,8},{8,9},{9,10},{10,1... | collective-permute-start | bytes 1572872 | tf_op jit(solution)/shard_map/ppermute | solution.py:16
  372.7 10.4 %collective-permute-start.4 = (s32[128]{0:T(128)S(1)}, s32[128]{0:T(128)S(1)}, u32[]{:S(2)}, u32[]{:S(2)}) collective-permute-start(s32[128]{0:T(128)S(1)} %collective-permute-done.3), channel_id=1, source_target_pairs={{0,1},{1,2},{2,3},{3,4},{4,5},{5,6},{6,7},{7,8},{8,9},{9,10},{10,1... | collective-permute-start | bytes 1544 | tf_op jit(solution)/shard_map/ppermute | solution.py:16
  383.1 7.3 %collective-permute-start.5 = (s32[128]{0:T(128)S(1)}, s32[128]{0:T(128)S(1)}, u32[]{:S(2)}, u32[]{:S(2)}) collective-permute-start(s32[128]{0:T(128)S(1)} %collective-permute-done.4), channel_id=1, source_target_pairs={{0,1},{1,2},{2,3},{3,4},{4,5},{5,6},{6,7},{7,8},{8,9},{9,10},{10,1... | collective-permute-start | bytes 1544 | tf_op jit(solution)/shard_map/ppermute | solution.py:16
  390.4 15.0 %collective-permute-start.6 = (s32[128]{0:T(128)S(1)}, s32[128]{0:T(128)S(1)}, u32[]{:S(2)}, u32[]{:S(2)}) collective-permute-start(s32[128]{0:T(128)S(1)} %collective-permute-done.5), channel_id=1, source_target_pairs={{0,1},{1,2},{2,3},{3,4},{4,5},{5,6},{6,7},{7,8},{8,9},{9,10},{10,1... | collective-permute-start | bytes 1544 | tf_op jit(solution)/shard_map/ppermute | solution.py:16
  401.0 17.1 %collective-permute-start.11 = (bf16[128,2048]{0,1:T(8,128)(2,1)}, bf16[128,2048]{0,1:T(8,128)(2,1)S(1)}, u32[]{:S(2)}, u32[]{:S(2)}) collective-permute-start(bf16[128,2048]{0,1:T(8,128)(2,1)} %collective-permute-done.10), channel_id=1, source_target_pairs={{0,1},{1,2},{2,3},{3,4},{4,5},{5,6},{6,7},{7,8},{8,9},{9,10},{10,1... | collective-permute-start | bytes 1572872 | tf_op jit(solution)/shard_map/ppermute | solution.py:16
  418.1 13.0 %copy-start.2 = (bf16[128,2048]{0,1:T(8,128)(2,1)}, bf16[128,2048]{0,1:T(8,128)(2,1)S(1)}, u32[]{:S(2)}) copy-start(bf16[128,2048]{0,1:T(8,128)(2,1)S(1)} %collective-permute-done.11) | copy-start | bytes 1572868
  418.1 13.0 %collective-permute-start.12 = (bf16[128,2048]{0,1:T(8,128)(2,1)S(1)}, bf16[128,2048]{0,1:T(8,128)(2,1)}, u32[]{:S(2)}, u32[]{:S(2)}) collective-permute-start(bf16[128,2048]{0,1:T(8,128)(2,1)S(1)} %collective-permute-done.11), channel_id=1, source_target_pairs={{0,1},{1,2},{2,3},{3,4},{4,5},{5,6},{6,7},{7,8},{8,9},{9,10},{10,1... | collective-permute-start | bytes 1572872 | tf_op jit(solution)/shard_map/ppermute | solution.py:16
  431.2 60.8 %collective-permute-start.13 = (bf16[128,2048]{0,1:T(8,128)(2,1)}, bf16[128,2048]{0,1:T(8,128)(2,1)S(1)}, u32[]{:S(2)}, u32[]{:S(2)}) collective-permute-start(bf16[128,2048]{0,1:T(8,128)(2,1)} %collective-permute-done.12), channel_id=1, source_target_pairs={{0,1},{1,2},{2,3},{3,4},{4,5},{5,6},{6,7},{7,8},{8,9},{9,10},{10,1... | collective-permute-start | bytes 1572872 | tf_op jit(solution)/shard_map/ppermute | solution.py:16
  467.5 8.5 %copy-start.3 = (bf16[128,2048]{0,1:T(8,128)(2,1)S(1)}, bf16[128,2048]{0,1:T(8,128)(2,1)}, u32[]{:S(2)}) copy-start(bf16[128,2048]{0,1:T(8,128)(2,1)} %copy-done.2) | copy-start | bytes 1572868
  508.2 6.4 %copy-start.1 = (bf16[128,8,8,128]{3,0,2,1:T(8,128)(2,1)S(1)}, bf16[128,8,8,128]{3,0,2,1:T(8,128)(2,1)}, u32[]{:S(2)}) copy-start(bf16[128,8,8,128]{3,0,2,1:T(8,128)(2,1)} %copy.138) | copy-start | bytes 6291460
  521.9 5.7 copy-start
  546.4 5.7 copy-start
Sparse Core Ops, SparseCore 0:
  9.0 350.6 all-gather.2
where the time goes:
time: 589 us; the launch traced here: 581 us
  blocking collectives  292 us (50%)
  matrix products  81.7 us (14%)
  waiting for transfers between devices  57.2 us (10%)
  starting transfers between devices  55 us (9%)
  local copies, waits for them, and re-layouts  41.4 us (7%)
  other arithmetic  31.8 us (5%)
  between operations  18.9 us (3%)
    all_gather x1, blocking collectives, on_device(): plan = lax.all_gather(tile_plan, ('prompt', 'resp'), axis=0, tiled=True)  292 us
    dot_general x10, matrix products, absorb(): jnp.einsum('luem,mut->luet', attention_weight.astype(jnp.bfloat16), value...  65.2 us
    ppermute x14, waiting for transfers between devices, passed_along(): lax.ppermute(value, axis, [(source, source + steps) for source in range(f...  56.4 us
    ppermute x14, starting transfers between devices, passed_along(): lax.ppermute(value, axis, [(source, source + steps) for source in range(f...  55 us
    reduce_sum x10, other arithmetic, absorb(): total = total * factor + jnp.sum(attention_weight, axis=-1)  21.7 us
    dot_general x10, matrix products, absorb(): jnp.einsum('wcpo,lco->wcpl', query_head_rows, key_vectors, preferred_elem...  16.5 us
  transfers between devices with their start and end apart: 15, of which 7 were waited for; matrix products, arithmetic and copies ran while one was open for 14% of the time, Pallas kernels for 0%

commit v1 on v0

--- a/solution.py
+++ b/solution.py
@@ -1,3 +1,4 @@
+import functools
 import math
 import jax
 import jax.numpy as jnp
@@ -8,6 +9,19 @@
 KVH = 8
 HD = 128
 NEG_FILL = -1e30
+
+
+def report_masks_by_axis(frame, which_dim):
+    state_now = jnp.concatenate(
+        lax.all_to_all(
+            jnp.stack([frame] * lax.axis_size(("prompt", "resp"))), ("prompt", "resp"), 0, 0
+        ),
+        axis=which_dim,
+    )
+    return state_now
+
+
+_turn_members_all = functools.partial(report_masks_by_axis, which_dim=0)
 
 
 def passed_along(value, axis, steps):
@@ -91,7 +105,7 @@
     n_prompt = lax.axis_size("prompt")
     state = carry
     tiles = lax.all_gather(prefix_kv, ("prompt", "resp"), axis=0, tiled=True)
-    plan = lax.all_gather(tile_plan, ("prompt", "resp"), axis=0, tiled=True)
+    plan = _turn_members_all(tile_plan)
     count = tiles.shape[0]
     tile = tiles.shape[1]
     count = count // n_prompt

time: 589 us -> 485 us (0.82)
  the two profiles are of different devices: /device:TPU:89 before, /device:TPU:17 now
where the time goes in v1:
time: 485 us; the launch traced here: 477 us
  waiting for transfers between devices  266 us (55%)
  matrix products  66.8 us (14%)
  starting transfers between devices  48.4 us (10%)
  local copies, waits for them, and re-layouts  43.4 us (9%)
  other arithmetic  30.7 us (6%)
  between operations  19 us (4%)
    all_gather x1, waiting for transfers between devices, on_device(): tiles = lax.all_gather(prefix_kv, ('prompt', 'resp'), axis=0, tiled=True)  178 us
    ppermute x14, waiting for transfers between devices, passed_along(): lax.ppermute(value, axis, [(source, source + steps) for source in range(f...  86.8 us
    dot_general x8, matrix products, absorb(): jnp.einsum('luem,mut->luet', attention_weight.astype(jnp.bfloat16), value...  53.1 us
    ppermute x14, starting transfers between devices, passed_along(): lax.ppermute(value, axis, [(source, source + steps) for source in range(f...  30.7 us
    all_to_all x1, starting transfers between devices, report_masks_by_axis(): lax.all_to_all(jnp.stack([frame] * lax.axis_size(('prompt', 'resp'))), ('...  17.7 us
    reduce_sum x8, other arithmetic, absorb(): total = total * factor + jnp.sum(attention_weight, axis=-1)  17.2 us
    dot_general x8, matrix products, absorb(): jnp.einsum('wcpo,lco->wcpl', query_head_rows, key_vectors, preferred_elem...  13.7 us
  transfers between devices with their start and end apart: 16, of which 11 were waited for; matrix products, arithmetic and copies ran while one was open for 14% of the time, Pallas kernels for 0%

profile of v1, /device:TPU:17, one launch (start us, length us, event | category | flops | bytes accessed | tf_op | source)
XLA Modules:
  0.0 476.7 jit_solution(2891109789438799764)
XLA Ops:
  12.1 14.2 %collective-permute-done.7 = bf16[128,2048]{0,1:T(8,128)(2,1)S(1)} collective-permute-done((bf16[128,2048]{0,1:T(8,128)(2,1)S(1)}, bf16[128,2048]{0,1:T(8,128)(2,1)S(1)}, u32[]{:S(2)}, u32[]{:S(2)}) %collective-permute-start.7) | collective-permute-done | bytes 524320 | tf_op jit(solution)/shard_map/ppermute | solution.py:30
  28.2 15.0 %collective-permute-done.8 = bf16[128,2048]{0,1:T(8,128)(2,1)} collective-permute-done((bf16[128,2048]{0,1:T(8,128)(2,1)S(1)}, bf16[128,2048]{0,1:T(8,128)(2,1)}, u32[]{:S(2)}, u32[]{:S(2)}) %collective-permute-start.8) | collective-permute-done | bytes 524320 | tf_op jit(solution)/shard_map/ppermute | solution.py:30
  47.8 11.6 %collective-permute-done = s32[128]{0:T(128)S(1)} collective-permute-done((s32[128]{0:T(128)S(1)}, s32[128]{0:T(128)S(1)}, u32[]{:S(2)}, u32[]{:S(2)}) %collective-permute-start) | collective-permute-done | bytes 544 | tf_op jit(solution)/shard_map/ppermute | solution.py:30
  61.3 5.4 %collective-permute-done.1 = s32[128]{0:T(128)S(1)} collective-permute-done((s32[128]{0:T(128)S(1)}, s32[128]{0:T(128)S(1)}, u32[]{:S(2)}, u32[]{:S(2)}) %collective-permute-start.1) | collective-permute-done | bytes 544 | tf_op jit(solution)/shard_map/ppermute | solution.py:30
  68.6 5.4 %collective-permute-done.2 = s32[128]{0:T(128)S(1)} collective-permute-done((s32[128]{0:T(128)S(1)}, s32[128]{0:T(128)S(1)}, u32[]{:S(2)}, u32[]{:S(2)}) %collective-permute-start.2) | collective-permute-done | bytes 544 | tf_op jit(solution)/shard_map/ppermute | solution.py:30
  75.9 5.4 %collective-permute-done.3 = s32[128]{0:T(128)S(1)} collective-permute-done((s32[128]{0:T(128)S(1)}, s32[128]{0:T(128)S(1)}, u32[]{:S(2)}, u32[]{:S(2)}) %collective-permute-start.3) | collective-permute-done | bytes 544 | tf_op jit(solution)/shard_map/ppermute | solution.py:30
  84.6 17.7 %all-to-all-start = ((s32[128,4,2]{1,2,0:T(2,128)}), s32[128,4,2]{1,2,0:T(2,128)S(1)}, u32[]{:S(2)}, u32[]{:S(2)}) async-start(s32[128,4,2]{1,2,0:T(2,128)} %stack.2), calls=%async_computation | async-start | bytes 262144 | tf_op jit(solution)/shard_map/all_to_all | solution.py:16
  123.2 13.9 %collective-permute-done.10 = bf16[128,2048]{0,1:T(8,128)(2,1)S(1)} collective-permute-done((bf16[128,2048]{0,1:T(8,128)(2,1)S(1)}, bf16[128,2048]{0,1:T(8,128)(2,1)S(1)}, u32[]{:S(2)}, u32[]{:S(2)}) %collective-permute-start.10) | collective-permute-done | bytes 524320 | tf_op jit(solution)/shard_map/ppermute | solution.py:30
  140.3 12.6 %collective-permute-done.11 = bf16[128,2048]{0,1:T(8,128)(2,1)} collective-permute-done((bf16[128,2048]{0,1:T(8,128)(2,1)S(1)}, bf16[128,2048]{0,1:T(8,128)(2,1)}, u32[]{:S(2)}, u32[]{:S(2)}) %collective-permute-start.11) | collective-permute-done | bytes 524320 | tf_op jit(solution)/shard_map/ppermute | solution.py:30
  174.6 9.1 %conditional.8 = ((f32[128,8,8]{0,2,1:T(8,128)S(1)}, f32[128,8,8]{0,2,1:T(8,128)S(1)}, f32[128,8,8,128]{3,0,2,1:T(8,128)})) conditional(s32[]{:T(128)} %convert_element_type.71, (f32[128,8,8]{0,2,1:T(8,128)S(1)}, f32[128,8,8]{0,2,1:T(8,128)S(1)}, f32[128,8,8,128]{3,0,2,1:T(8,128)}) %tuple.61, (pred[128,128]{0,1:T(8,128)(4,1)}, ...), branch_computations={%region_9.10_spmd, %region_10.13_spmd} | conditional | flops 552615936 | bytes 25280572 | solution.py:102
  178.6 5.2 %bitcast_add_fusion = f32[128,8,8,128]{3,0,2,1:T(8,128)} fusion(f32[128,8,8,128]{3,0,2,1:T(8,128)} %get-tuple-element.202, bf16[128,8,128,1]{0,2,3,1:T(8,128)(2,1)S(1)} %bitcast.266, f32[8,128,128,8]{2,1,3,0:T(8,128)S(1)} %get-tuple-element.494, f32[128,8,8]{0,2,1:T(8,128)S(1)} %get-tuple-element.474, f32[128,8,8]{0,2,1:T(8,128)S(1)} %max.17, ...), kind=kOutput, calls=%fused_computation.2 | convolution fusion | flops 275775488 | bytes 12926976 | tf_op jit(solution)/shard_map/cond/branch_1_fun/luem,mut->luet/dot_general | solution.py:46
  183.8 8.9 %conditional.9 = ((f32[128,8,8]{0,2,1:T(8,128)S(1)}, f32[128,8,8]{0,2,1:T(8,128)S(1)}, f32[128,8,8,128]{3,0,2,1:T(8,128)})) conditional(s32[]{:T(128)} %convert_element_type.70, (f32[128,8,8]{0,2,1:T(8,128)S(1)}, f32[128,8,8]{0,2,1:T(8,128)S(1)}, f32[128,8,8,128]{3,0,2,1:T(8,128)}) %get-tuple-element.662, (pred[128,128]{0,1:T(8,128)(4,1)S(1)}, ...), branch_computations={%region_13.14_spmd, %region_14.17_spmd} | conditional | flops 552615936 | bytes 25215008 | solution.py:102
  187.4 5.2 %bitcast_add_fusion.1 = f32[128,8,8,128]{3,0,2,1:T(8,128)} fusion(f32[128,8,8,128]{3,0,2,1:T(8,128)} %get-tuple-element.208, bf16[128,8,128,1]{0,2,3,1:T(8,128)(2,1)S(1)} %bitcast.267, f32[8,128,128,8]{2,1,3,0:T(8,128)S(1)} %get-tuple-element.498, f32[128,8,8]{0,2,1:T(8,128)S(1)} %get-tuple-element.476, f32[128,8,8]{0,2,1:T(8,128)S(1)} %max.18, ...), kind=kOutput, calls=%fused_computation.18 | convolution fusion | flops 275775488 | bytes 12926976 | tf_op jit(solution)/shard_map/cond/branch_1_fun/luem,mut->luet/dot_general | solution.py:46
  192.7 7.4 %conditional.10 = ((f32[128,8,8]{0,2,1:T(8,128)S(1)}, f32[128,8,8]{0,2,1:T(8,128)S(1)}, f32[128,8,8,128]{3,0,2,1:T(8,128)})) conditional(s32[]{:T(128)} %convert_element_type.69, (f32[128,8,8]{0,2,1:T(8,128)S(1)}, f32[128,8,8]{0,2,1:T(8,128)S(1)}, f32[128,8,8,128]{3,0,2,1:T(8,128)}) %get-tuple-element.663, (pred[128,128]{0,1:T(8,128)(4,1)S(1)}, ...), branch_computations={%region_17.18_spmd, %region_18.21_spmd} | conditional | flops 552615936 | bytes 25215008 | solution.py:102
  194.8 5.2 %bitcast_add_fusion.2 = f32[128,8,8,128]{3,0,2,1:T(8,128)} fusion(f32[128,8,8,128]{3,0,2,1:T(8,128)} %get-tuple-element.214, bf16[128,8,128,1]{0,2,3,1:T(8,128)(2,1)S(1)} %bitcast.268, f32[8,128,128,8]{2,1,3,0:T(8,128)S(1)} %get-tuple-element.502, f32[128,8,8]{0,2,1:T(8,128)S(1)} %get-tuple-element.478, f32[128,8,8]{0,2,1:T(8,128)S(1)} %max.19, ...), kind=kOutput, calls=%fused_computation.34 | convolution fusion | flops 275775488 | bytes 12926976 | tf_op jit(solution)/shard_map/cond/branch_1_fun/luem,mut->luet/dot_general | solution.py:46
  200.0 8.4 %conditional.11 = ((f32[128,8,8]{0,2,1:T(8,128)S(1)}, f32[128,8,8]{0,2,1:T(8,128)S(1)}, f32[128,8,8,128]{3,0,2,1:T(8,128)})) conditional(s32[]{:T(128)} %convert_element_type.68, (f32[128,8,8]{0,2,1:T(8,128)S(1)}, f32[128,8,8]{0,2,1:T(8,128)S(1)}, f32[128,8,8,128]{3,0,2,1:T(8,128)}) %get-tuple-element.664, (pred[128,128]{0,1:T(8,128)(4,1)S(1)}, ...), branch_computations={%region_21.0_spmd, %region_22.25_spmd} | conditional | flops 552615936 | bytes 25215008 | solution.py:102
  203.2 5.3 %bitcast_add_fusion.3 = f32[128,8,8,128]{3,0,2,1:T(8,128)} fusion(f32[128,8,8,128]{3,0,2,1:T(8,128)} %get-tuple-element.220, bf16[128,8,128,1]{0,2,3,1:T(8,128)(2,1)S(1)} %bitcast.269, f32[8,128,128,8]{2,1,3,0:T(8,128)S(1)} %get-tuple-element.506, f32[128,8,8]{0,2,1:T(8,128)S(1)} %get-tuple-element.480, f32[128,8,8]{0,2,1:T(8,128)S(1)} %max.20, ...), kind=kOutput, calls=%fused_computation.50 | convolution fusion | flops 275775488 | bytes 12926976 | tf_op jit(solution)/shard_map/cond/branch_1_fun/luem,mut->luet/dot_general | solution.py:46
  208.4 8.6 %conditional.12 = ((f32[128,8,8]{0,2,1:T(8,128)S(1)}, f32[128,8,8]{0,2,1:T(8,128)S(1)}, f32[128,8,8,128]{3,0,2,1:T(8,128)})) conditional(s32[]{:T(128)} %convert_element_type.67, (f32[128,8,8]{0,2,1:T(8,128)S(1)}, f32[128,8,8]{0,2,1:T(8,128)S(1)}, f32[128,8,8,128]{3,0,2,1:T(8,128)}) %get-tuple-element.665, (pred[128,128]{0,1:T(8,128)(4,1)S(1)}, ...), branch_computations={%region_25.0_spmd, %region_26.29_spmd} | conditional | flops 552615936 | bytes 25215008 | solution.py:102
  211.8 5.2 %bitcast_add_fusion.4 = f32[128,8,8,128]{3,0,2,1:T(8,128)} fusion(f32[128,8,8,128]{3,0,2,1:T(8,128)} %get-tuple-element.226, bf16[128,8,128,1]{0,2,3,1:T(8,128)(2,1)S(1)} %bitcast.270, f32[8,128,128,8]{2,1,3,0:T(8,128)S(1)} %get-tuple-element.510, f32[128,8,8]{0,2,1:T(8,128)S(1)} %get-tuple-element.482, f32[128,8,8]{0,2,1:T(8,128)S(1)} %max.21, ...), kind=kOutput, calls=%fused_computation.66 | convolution fusion | flops 275775488 | bytes 12926976 | tf_op jit(solution)/shard_map/cond/branch_1_fun/luem,mut->luet/dot_general | solution.py:46
  217.3 178.4 %all-gather.2.cloned.1.call-done = bf16[512,8,2048]{2,1,0:T(8,128)(2,1)} async-done(((bf16[4,8,2048]{2,1,0:T(8,128)(2,1)}), bf16[512,8,2048]{2,1,0:T(8,128)(2,1)}) %all-gather.2.cloned.1.call-update) | async-done | bytes 16777232 | tf_op jit(solution)/shard_map/all_gather | solution.py:107
  395.7 8.7 %gather_fusion.1 = bf16[128,8,2048]{2,1,0:T(8,128)(2,1)} fusion(bf16[512,8,2048]{2,1,0:T(8,128)(2,1)} %all-gather.2.cloned.1.call-done, s32[1024]{0:T(1024)} %pad_clamp_fusion), kind=kCustom, calls=%fused_computation.1 | custom fusion | bytes 8389120 | tf_op jit(solution)/shard_map/gather | solution.py:113
  404.4 6.4 %copy.137 = bf16[2,512,2048]{1,2,0:T(8,128)(2,1)} copy(bf16[2,512,2048]{2,1,0:T(8,128)(2,1)} %bitcast.260) | data formatting | bytes 8388608 | tf_op jit(solution)/shard_map/while | solution.py:138
  410.8 49.1 %while.14 = (s32[]{:T(128)}, f32[128,8,8]{0,2,1:T(8,128)S(1)}, f32[128,8,8]{0,2,1:T(8,128)S(1)}, f32[128,8,8,128]{3,0,2,1:T(8,128)}, pred[2,512]{1,0:T(4,128)(4,...) while((s32[]{:T(128)}, f32[128,8,8]{0,2,1:T(8,128)S(1)}, ...), condition=%wide.region_44.45_spmd, body=%wide.region_38.44_spmd.sunk | while | flops 2204123648 | bytes 138940144 | solution.py:138
  412.1 23.2 %conditional.16 = ((f32[128,8,8]{0,2,1:T(8,128)S(1)}, f32[128,8,8]{0,2,1:T(8,128)S(1)}, f32[128,8,8,128]{3,0,2,1:T(8,128)})) conditional(s32[]{:T(128)} %convert_element_type.97, (f32[128,8,8]{0,2,1:T(8,128)S(1)}, f32[128,8,8]{0,2,1:T(8,128)S(1)}, f32[128,8,8,128]{3,0,2,1:T(8,128)}) %tuple.148, (pred[1,512]{1,0:T(4,128)(4,1)S(1)}, ...), branch_computations={%region_40.40_spmd, %region_41.43_spmd} | conditional | flops 2204123136 | bytes 138938944 | solution.py:136
  414.0 4.1 bitcast_reduce_fusion
  418.1 4.9 %fusion.87 = f32[128,8,8]{0,2,1:T(8,128)S(1)} fusion(f32[8,512,128,8]{2,1,3,0:T(8,128)S(1)} %get-tuple-element.522, f32[128,8,8]{0,2,1:T(8,128)S(1)} %max.24, pred[512]{0:T(512)(128)(4,1)S(1)} %reduce.1), kind=kLoop, calls=%fused_computation.120 | loop fusion | flops 20963328 | bytes 16843264 | tf_op jit(solution)/shard_map/while/body/eval_jaxpr/cond/branch_1_fun/reduce_sum | solution.py:45
  423.8 11.5 %bitcast_add_fusion.7 = f32[128,8,8,128]{3,0,2,1:T(8,128)} fusion(f32[128,8,8,128]{3,0,2,1:T(8,128)} %get-tuple-element.245, bf16[512,8,128,1]{0,2,3,1:T(8,128)(2,1)S(1)} %bitcast.259, f32[8,512,128,8]{2,1,3,0:T(8,128)} %copy-done, f32[128,8,8]{0,2,1:T(8,128)S(1)} %max.24, pred[512]{0:T(512)(128)(4,1)S(1)} %reduce.1, f32[128,8,8]{0,2,1:T(8,128)S(1)} %get-tuple-element.488), kind=kOutput, calls=%fused_computation.124 | convolution fusion | flops 1096810496 | bytes 26280448 | tf_op jit(solution)/shard_map/while/body/eval_jaxpr/cond/branch_1_fun/luem,mut->luet/dot_general | solution.py:46
  436.6 23.2 %conditional.16 = ((f32[128,8,8]{0,2,1:T(8,128)S(1)}, f32[128,8,8]{0,2,1:T(8,128)S(1)}, f32[128,8,8,128]{3,0,2,1:T(8,128)})) conditional(s32[]{:T(128)} %convert_element_type.97, (f32[128,8,8]{0,2,1:T(8,128)S(1)}, f32[128,8,8]{0,2,1:T(8,128)S(1)}, f32[128,8,8,128]{3,0,2,1:T(8,128)}) %tuple.148, (pred[1,512]{1,0:T(4,128)(4,1)S(1)}, ...), branch_computations={%region_40.40_spmd, %region_41.43_spmd} | conditional | flops 2204123136 | bytes 138938944 | solution.py:136
  438.6 4.1 bitcast_reduce_fusion
  442.7 4.9 %fusion.87 = f32[128,8,8]{0,2,1:T(8,128)S(1)} fusion(f32[8,512,128,8]{2,1,3,0:T(8,128)S(1)} %get-tuple-element.522, f32[128,8,8]{0,2,1:T(8,128)S(1)} %max.24, pred[512]{0:T(512)(128)(4,1)S(1)} %reduce.1), kind=kLoop, calls=%fused_computation.120 | loop fusion | flops 20963328 | bytes 16843264 | tf_op jit(solution)/shard_map/while/body/eval_jaxpr/cond/branch_1_fun/reduce_sum | solution.py:45
  448.4 11.5 %bitcast_add_fusion.7 = f32[128,8,8,128]{3,0,2,1:T(8,128)} fusion(f32[128,8,8,128]{3,0,2,1:T(8,128)} %get-tuple-element.245, bf16[512,8,128,1]{0,2,3,1:T(8,128)(2,1)S(1)} %bitcast.259, f32[8,512,128,8]{2,1,3,0:T(8,128)} %copy-done, f32[128,8,8]{0,2,1:T(8,128)S(1)} %max.24, pred[512]{0:T(512)(128)(4,1)S(1)} %reduce.1, f32[128,8,8]{0,2,1:T(8,128)S(1)} %get-tuple-element.488), kind=kOutput, calls=%fused_computation.124 | convolution fusion | flops 1096810496 | bytes 26280448 | tf_op jit(solution)/shard_map/while/body/eval_jaxpr/cond/branch_1_fun/luem,mut->luet/dot_general | solution.py:46
  465.4 4.2 convert_element_type.74
  (111 shorter events, 89.4 us)
Async XLA Ops:
  6.5 389.2 %all-gather.2.cloned.1.call-start = ((), (), s32[]{:S(2)}) async-start(), calls=%async_computation.1 | async-start | bytes 16908288 | tf_op jit(solution)/shard_map/all_gather | solution.py:107
  8.6 17.8 %collective-permute-start.7 = (bf16[128,2048]{0,1:T(8,128)(2,1)S(1)}, bf16[128,2048]{0,1:T(8,128)(2,1)S(1)}, u32[]{:S(2)}, u32[]{:S(2)}) collective-permute-start(bf16[128,2048]{0,1:T(8,128)(2,1)S(1)} %bitcast.263), channel_id=1, source_target_pairs={{0,1},{1,2},{2,3},{3,4},{4,5},{5,6},{6,7},{7,8},{8,9},{9,10},{10,1... | collective-permute-start | bytes 1572872 | tf_op jit(solution)/shard_map/ppermute | solution.py:30
  26.3 79.3 %copy-start.3 = (bf16[128,2048]{0,1:T(8,128)(2,1)}, bf16[128,2048]{0,1:T(8,128)(2,1)S(1)}, u32[]{:S(2)}) copy-start(bf16[128,2048]{0,1:T(8,128)(2,1)S(1)} %collective-permute-done.7) | copy-start | bytes 1572868
  26.3 16.9 %collective-permute-start.8 = (bf16[128,2048]{0,1:T(8,128)(2,1)S(1)}, bf16[128,2048]{0,1:T(8,128)(2,1)}, u32[]{:S(2)}, u32[]{:S(2)}) collective-permute-start(bf16[128,2048]{0,1:T(8,128)(2,1)S(1)} %collective-permute-done.7), channel_id=1, source_target_pairs={{0,1},{1,2},{2,3},{3,4},{4,5},{5,6},{6,7},{7,8},{8,9},{9,10},{10,1... | collective-permute-start | bytes 1572872 | tf_op jit(solution)/shard_map/ppermute | solution.py:30
  43.3 77.2 %collective-permute-start.9 = (bf16[128,2048]{0,1:T(8,128)(2,1)}, bf16[128,2048]{0,1:T(8,128)(2,1)S(1)}, u32[]{:S(2)}, u32[]{:S(2)}) collective-permute-start(bf16[128,2048]{0,1:T(8,128)(2,1)} %collective-permute-done.8), channel_id=1, source_target_pairs={{0,1},{1,2},{2,3},{3,4},{4,5},{5,6},{6,7},{7,8},{8,9},{9,10},{10,1... | collective-permute-start | bytes 1572872 | tf_op jit(solution)/shard_map/ppermute | solution.py:30
  45.8 13.6 %collective-permute-start = (s32[128]{0:T(128)S(1)}, s32[128]{0:T(128)S(1)}, u32[]{:S(2)}, u32[]{:S(2)}) collective-permute-start(s32[128]{0:T(128)S(1)} %add_bitcast_fusion), channel_id=1, source_target_pairs={{0,1},{1,2},{2,3},{3,4},{4,5},{5,6},{6,7},{7,8},{8,9},{9,10},{10,1... | collective-permute-start | bytes 1544 | tf_op jit(solution)/shard_map/ppermute | solution.py:30
  59.4 7.3 %collective-permute-start.1 = (s32[128]{0:T(128)S(1)}, s32[128]{0:T(128)S(1)}, u32[]{:S(2)}, u32[]{:S(2)}) collective-permute-start(s32[128]{0:T(128)S(1)} %collective-permute-done), channel_id=1, source_target_pairs={{0,1},{1,2},{2,3},{3,4},{4,5},{5,6},{6,7},{7,8},{8,9},{9,10},{10,1... | collective-permute-start | bytes 1544 | tf_op jit(solution)/shard_map/ppermute | solution.py:30
  66.7 7.3 %collective-permute-start.2 = (s32[128]{0:T(128)S(1)}, s32[128]{0:T(128)S(1)}, u32[]{:S(2)}, u32[]{:S(2)}) collective-permute-start(s32[128]{0:T(128)S(1)} %collective-permute-done.1), channel_id=1, source_target_pairs={{0,1},{1,2},{2,3},{3,4},{4,5},{5,6},{6,7},{7,8},{8,9},{9,10},{10,1... | collective-permute-start | bytes 1544 | tf_op jit(solution)/shard_map/ppermute | solution.py:30
  74.0 7.3 %collective-permute-start.3 = (s32[128]{0:T(128)S(1)}, s32[128]{0:T(128)S(1)}, u32[]{:S(2)}, u32[]{:S(2)}) collective-permute-start(s32[128]{0:T(128)S(1)} %collective-permute-done.2), channel_id=1, source_target_pairs={{0,1},{1,2},{2,3},{3,4},{4,5},{5,6},{6,7},{7,8},{8,9},{9,10},{10,1... | collective-permute-start | bytes 1544 | tf_op jit(solution)/shard_map/ppermute | solution.py:30
  81.3 20.9 %collective-permute-start.4 = (s32[128]{0:T(128)S(1)}, s32[128]{0:T(128)S(1)}, u32[]{:S(2)}, u32[]{:S(2)}) collective-permute-start(s32[128]{0:T(128)S(1)} %collective-permute-done.3), channel_id=1, source_target_pairs={{0,1},{1,2},{2,3},{3,4},{4,5},{5,6},{6,7},{7,8},{8,9},{9,10},{10,1... | collective-permute-start | bytes 1544 | tf_op jit(solution)/shard_map/ppermute | solution.py:30
  84.6 78.6 %all-to-all-start = ((s32[128,4,2]{1,2,0:T(2,128)}), s32[128,4,2]{1,2,0:T(2,128)S(1)}, u32[]{:S(2)}, u32[]{:S(2)}) async-start(s32[128,4,2]{1,2,0:T(2,128)} %stack.2), calls=%async_computation | async-start | bytes 262144 | tf_op jit(solution)/shard_map/all_to_all | solution.py:16
  102.3 9.2 %collective-permute-start.5 = (s32[128]{0:T(128)S(1)}, s32[128]{0:T(128)S(1)}, u32[]{:S(2)}, u32[]{:S(2)}) collective-permute-start(s32[128]{0:T(128)S(1)} %collective-permute-done.4), channel_id=1, source_target_pairs={{0,1},{1,2},{2,3},{3,4},{4,5},{5,6},{6,7},{7,8},{8,9},{9,10},{10,1... | collective-permute-start | bytes 1544 | tf_op jit(solution)/shard_map/ppermute | solution.py:30
  111.5 7.3 %collective-permute-start.6 = (s32[128]{0:T(128)S(1)}, s32[128]{0:T(128)S(1)}, u32[]{:S(2)}, u32[]{:S(2)}) collective-permute-start(s32[128]{0:T(128)S(1)} %collective-permute-done.5), channel_id=1, source_target_pairs={{0,1},{1,2},{2,3},{3,4},{4,5},{5,6},{6,7},{7,8},{8,9},{9,10},{10,1... | collective-permute-start | bytes 1544 | tf_op jit(solution)/shard_map/ppermute | solution.py:30
  120.4 16.6 %collective-permute-start.10 = (bf16[128,2048]{0,1:T(8,128)(2,1)S(1)}, bf16[128,2048]{0,1:T(8,128)(2,1)S(1)}, u32[]{:S(2)}, u32[]{:S(2)}) collective-permute-start(bf16[128,2048]{0,1:T(8,128)(2,1)S(1)} %collective-permute-done.9), channel_id=1, source_target_pairs={{0,1},{1,2},{2,3},{3,4},{4,5},{5,6},{6,7},{7,8},{8,9},{9,10},{10,1... | collective-permute-start | bytes 1572872 | tf_op jit(solution)/shard_map/ppermute | solution.py:30
  137.1 21.7 %copy-start.2 = (bf16[128,2048]{0,1:T(8,128)(2,1)}, bf16[128,2048]{0,1:T(8,128)(2,1)S(1)}, u32[]{:S(2)}) copy-start(bf16[128,2048]{0,1:T(8,128)(2,1)S(1)} %collective-permute-done.10) | copy-start | bytes 1572868
  137.1 15.9 %collective-permute-start.11 = (bf16[128,2048]{0,1:T(8,128)(2,1)S(1)}, bf16[128,2048]{0,1:T(8,128)(2,1)}, u32[]{:S(2)}, u32[]{:S(2)}) collective-permute-start(bf16[128,2048]{0,1:T(8,128)(2,1)S(1)} %collective-permute-done.10), channel_id=1, source_target_pairs={{0,1},{1,2},{2,3},{3,4},{4,5},{5,6},{6,7},{7,8},{8,9},{9,10},{10,1... | collective-permute-start | bytes 1572872 | tf_op jit(solution)/shard_map/ppermute | solution.py:30
  152.9 15.2 %collective-permute-start.12 = (bf16[128,2048]{0,1:T(8,128)(2,1)}, bf16[128,2048]{0,1:T(8,128)(2,1)}, u32[]{:S(2)}, u32[]{:S(2)}) collective-permute-start(bf16[128,2048]{0,1:T(8,128)(2,1)} %collective-permute-done.11), channel_id=1, source_target_pairs={{0,1},{1,2},{2,3},{3,4},{4,5},{5,6},{6,7},{7,8},{8,9},{9,10},{10,1... | collective-permute-start | bytes 1572872 | tf_op jit(solution)/shard_map/ppermute | solution.py:30
  168.1 48.9 %collective-permute-start.13 = (bf16[128,2048]{0,1:T(8,128)(2,1)}, bf16[128,2048]{0,1:T(8,128)(2,1)S(1)}, u32[]{:S(2)}, u32[]{:S(2)}) collective-permute-start(bf16[128,2048]{0,1:T(8,128)(2,1)} %collective-permute-done.12), channel_id=1, source_target_pairs={{0,1},{1,2},{2,3},{3,4},{4,5},{5,6},{6,7},{7,8},{8,9},{9,10},{10,1... | collective-permute-start | bytes 1572872 | tf_op jit(solution)/shard_map/ppermute | solution.py:30
  174.6 9.1 %copy-start.4 = (pred[128,128]{0,1:T(8,128)(4,1)S(1)}, pred[128,128]{0,1:T(8,128)(4,1)}, u32[]{:S(2)}) copy-start(pred[128,128]{0,1:T(8,128)(4,1)} %get-tuple-element.532) | copy-start | bytes 49156
  174.7 2.6 copy-start.5
  404.4 6.4 %copy-start.1 = (bf16[128,8,8,128]{3,0,2,1:T(8,128)(2,1)S(1)}, bf16[128,8,8,128]{3,0,2,1:T(8,128)(2,1)}, u32[]{:S(2)}) copy-start(bf16[128,8,8,128]{3,0,2,1:T(8,128)(2,1)} %copy.138) | copy-start | bytes 6291460
  418.1 5.7 %copy-start = (f32[8,512,128,8]{2,1,3,0:T(8,128)}, f32[8,512,128,8]{2,1,3,0:T(8,128)S(1)}, u32[]{:S(2)}) copy-start(f32[8,512,128,8]{2,1,3,0:T(8,128)S(1)} %get-tuple-element.522) | copy-start | bytes 50331652 | tf_op jit(solution)/shard_map/while/body/eval_jaxpr/cond
  442.6 5.7 %copy-start = (f32[8,512,128,8]{2,1,3,0:T(8,128)}, f32[8,512,128,8]{2,1,3,0:T(8,128)S(1)}, u32[]{:S(2)}) copy-start(f32[8,512,128,8]{2,1,3,0:T(8,128)S(1)} %get-tuple-element.522) | copy-start | bytes 50331652 | tf_op jit(solution)/shard_map/while/body/eval_jaxpr/cond
Sparse Core Ops, SparseCore 0:
  9.0 386.6 all-gather.1
